TPU v7x, 256 devices: a whole 4x4x8 slice. The times are simulated.
256 devices in a mesh: head: 4 (over x), blk: 64 (over y, z, core).
Axes of the slice: x: 4, y: 4, z: 8, core: 2. Of those that a mesh axis runs over, the one named last changes fastest.
Arguments:
- doc_x: bfloat16 [65536, 1024], P('blk'), may hold values from -6 to 6
- doc_seg: int32 [65536], P('blk'), may hold values from 0 to 1023, as said below
- doc_query: int32 [1024], replicated, may hold values from 0 to 7
- doc_var: int32 [65536], P('blk'), may hold values from 0 to 7
- query_len: int32 [8], replicated, may hold values from 256 to 4096, as said below
- block_perm: int32 [64], replicated, may hold values from 0 to 63, each once
- cache_k: bfloat16 [32768, 1024], P('blk', 'head'), may hold values from -164 to 164
- cache_v: bfloat16 [32768, 1024], P('blk', 'head'), may hold values from -6 to 6
- cache_var: int32 [32768], P('blk'), may hold values from 0 to 7
- w_query: bfloat16 [1024, 1024], P(None, 'head'), may hold values from -0.1875 to 0.1875
- w_key: bfloat16 [1024, 1024], P(None, 'head'), may hold values from -0.5 to 0.5
- w_value: bfloat16 [1024, 1024], P(None, 'head'), may hold values from -0.1875 to 0.1875
- w_out: bfloat16 [1024, 1024], P('head'), may hold values from -0.1875 to 0.1875
- var_bias: float32 [2, 16], P(None, 'head'), may hold values from -1 to 1
- norm_gain: float32 [1024], replicated, may hold values from 0.1 to 1.9
- readout: float32 [1024], replicated, may hold values from -1.5 to 1.5
Outputs:
- update: float32 [65536, 1024], P('blk', 'head')
- pooled: float32 [1024], P('blk')
Inputs may be any that keep to these rules, and one draw needn't show every extreme that they name: `doc_seg`: index i of blk holds documents i * 16 to (i + 1) * 16 - 1 whole; its 1024 tokens form 8 runs of 128 tokens, run j holding its documents 2j and 2j + 1, both of one query, and the 8 runs of one index belong to 8 different queries. query_len[0] = 4096.
All inputs are finite; a program needn't handle non-finite values.
Results may differ from a plain program's by a relative error of at most 0.012.
The roundings to bfloat16 on the way count: a program that leaves them out, or rounds other values in their place, can miss the bound.
Values may be sent and summed in bfloat16 or wider, within the bound.
A program may use at most 128 MiB of HBM per device.

v0:
```python
import jax
import jax.numpy as jnp
from jax import lax
from jax.sharding import PartitionSpec as P

D = 1024
DH = 64
QUERIES = 8


def rotary(projected, positions):
    row_count = projected.shape[0]
    head_count = projected.shape[1] // DH
    half_size = DH // 2
    shaped = projected.reshape(row_count, head_count, DH)
    frequency = 10000.0 ** (-jnp.arange(half_size, dtype=jnp.float32) / half_size)
    angles = positions.astype(jnp.float32)[:, None] * frequency[None, :]
    cosine = jnp.cos(angles)[:, None, :]
    sine_part = jnp.sin(angles)[:, None, :]
    first_half = shaped[:, :, :half_size]
    second_half = shaped[:, :, half_size:]
    turned = jnp.concatenate(
        [
            first_half * cosine - second_half * sine_part,
            second_half * cosine + first_half * sine_part,
        ],
        axis=2,
    )
    return turned.reshape(row_count, head_count * DH)


def softmax_part(scores, allowed):
    scores = jnp.where(allowed, scores, -1e30)
    peak = jnp.max(scores, axis=-1)
    weights = jnp.where(allowed, jnp.exp(scores - peak[..., None]), 0.0)
    return (peak, jnp.sum(weights, axis=-1), weights.astype(jnp.bfloat16))


def cache_part(
    recv_q, recv_var, cache_keys, cache_values, cache_var, row_valid, bias_same, bias_other
):
    source_count = recv_q.shape[0]
    item_count = recv_q.shape[1]
    col_count = recv_q.shape[2]
    head_count = cache_keys.shape[1]
    total_rows = source_count * item_count
    block_rows = 512
    block_count = total_rows // block_rows
    flat_q = recv_q.reshape(block_count, block_rows, head_count, DH)
    flat_var = recv_var.reshape(block_count, block_rows).astype(jnp.int32)

    def one_block(block_inputs):
        block_q, block_var = block_inputs
        scores = (
            jnp.einsum("thd,rhd->htr", block_q, cache_keys, preferred_element_type=jnp.float32)
            * 0.125
        )
        scores = scores + jnp.where(
            (block_var[:, None] == cache_var[None, :])[None], bias_same, bias_other
        )
        allowed = jnp.broadcast_to(row_valid[None, None, :], scores.shape)
        peak, total_weight, weights = softmax_part(scores, allowed)
        mixed = jnp.einsum(
            "htr,rhd->thd", weights, cache_values, preferred_element_type=jnp.float32
        )
        return (peak.T, total_weight.T, mixed.reshape(block_rows, col_count))

    maxima, totals, sums = lax.map(one_block, (flat_q, flat_var))
    return (
        maxima.reshape(source_count, item_count, head_count),
        totals.reshape(source_count, item_count, head_count),
        sums.reshape(source_count, item_count, col_count),
    )


def body(
    doc_x,
    doc_seg,
    doc_query,
    doc_var,
    query_len,
    block_perm,
    cache_k,
    cache_v,
    cache_var,
    w_query,
    w_key,
    w_value,
    w_out,
    var_bias,
    norm_gain,
    readout,
):
    row_count = doc_x.shape[0]
    col_count = w_query.shape[1]
    head_count = col_count // DH
    cache_count = cache_k.shape[0]
    blk_count = lax.axis_size("blk")
    blk_index = lax.axis_index("blk")
    head_index = lax.axis_index("head")
    blocks_each = blk_count // QUERIES
    slot_count = QUERIES
    slot_rows = row_count // slot_count
    doc_count = 2 * slot_count
    first_doc = blk_index * doc_count
    local_seg = doc_seg - first_doc
    member = (local_seg[:, None] == jnp.arange(doc_count, dtype=jnp.int32)[None, :]).astype(
        jnp.int32
    )
    lengths = jnp.sum(member, axis=0)
    starts = jnp.cumsum(lengths) - lengths
    first_pos = jnp.dot(member, starts)
    own_docs_query = lax.dynamic_slice_in_dim(doc_query, first_doc, doc_count)
    query_table = (own_docs_query[:, None] == jnp.arange(QUERIES, dtype=jnp.int32)[None, :]).astype(
        jnp.int32
    )
    doc_len = jnp.sum(query_table * query_len[None, :], axis=1)
    tok_len = jnp.dot(member, doc_len)
    positions = tok_len + jnp.arange(row_count, dtype=jnp.int32) - first_pos
    query_rot = rotary(
        jnp.dot(doc_x, w_query, preferred_element_type=jnp.float32), positions
    ).astype(jnp.bfloat16)
    key_rot = rotary(jnp.dot(doc_x, w_key, preferred_element_type=jnp.float32), positions).astype(
        jnp.bfloat16
    )
    value_proj = jnp.dot(doc_x, w_value, preferred_element_type=jnp.float32).astype(jnp.bfloat16)
    bias_same = var_bias[0][:, None, None]
    bias_other = var_bias[1][:, None, None]
    shaped_q = query_rot.reshape(slot_count, slot_rows, head_count, DH)
    shaped_k = key_rot.reshape(slot_count, slot_rows, head_count, DH)
    shaped_v = value_proj.reshape(slot_count, slot_rows, head_count, DH)
    slot_seg = local_seg.reshape(slot_count, slot_rows)
    slot_var = doc_var.reshape(slot_count, slot_rows)
    self_scores = (
        jnp.einsum("gthd,gshd->ghts", shaped_q, shaped_k, preferred_element_type=jnp.float32)
        * 0.125
    )
    self_scores = self_scores + jnp.where(
        (slot_var[:, :, None] == slot_var[:, None, :])[:, None], bias_same[None], bias_other[None]
    )
    self_allowed = (slot_seg[:, :, None] == slot_seg[:, None, :])[:, None]
    self_peak, self_total, self_weights = softmax_part(self_scores, self_allowed)
    self_sum = jnp.einsum(
        "ghts,gshd->gthd", self_weights, shaped_v, preferred_element_type=jnp.float32
    )
    self_peak = self_peak.transpose(0, 2, 1)
    self_total = self_total.transpose(0, 2, 1)
    slot_query = own_docs_query.reshape(slot_count, 2)[:, 0]
    block_query = block_perm // blocks_each
    slot_match = block_query[:, None] == slot_query[None, :]
    slot_pick = jnp.sum(
        slot_match.astype(jnp.int32) * jnp.arange(slot_count, dtype=jnp.int32)[None, :], axis=1
    )
    send_q = jnp.take(query_rot.reshape(slot_count, slot_rows, col_count), slot_pick, axis=0)
    send_var = jnp.take(slot_var, slot_pick, axis=0).astype(jnp.bfloat16)
    my_block = lax.dynamic_slice_in_dim(block_perm, blk_index, 1)[0]
    my_query = my_block // blocks_each
    first_row = my_block % blocks_each * cache_count
    my_len = lax.dynamic_slice_in_dim(query_len, my_query, 1)[0]
    row_valid = first_row + jnp.arange(cache_count, dtype=jnp.int32) < my_len
    cache_keys = cache_k.reshape(cache_count, head_count, DH)
    cache_values = cache_v.reshape(cache_count, head_count, DH)
    recv_q, recv_var = (
        lax.all_to_all(send_q, "blk", split_axis=0, concat_axis=0, tiled=True),
        lax.all_to_all(send_var, "blk", split_axis=0, concat_axis=0, tiled=True),
    )
    maxima, totals, sums = cache_part(
        recv_q, recv_var, cache_keys, cache_values, cache_var, row_valid, bias_same, bias_other
    )
    got_max, got_total, got_sum = (
        lax.all_to_all(maxima, "blk", split_axis=0, concat_axis=0, tiled=True),
        lax.all_to_all(totals, "blk", split_axis=0, concat_axis=0, tiled=True),
        lax.all_to_all(sums, "blk", split_axis=0, concat_axis=0, tiled=True),
    )
    match_float = slot_match.astype(jnp.float32)
    spread_max = jnp.where(slot_match[:, :, None, None], got_max[:, None], -1e30)
    cache_peak = jnp.max(spread_max, axis=0)
    peak = jnp.maximum(cache_peak, self_peak)
    device_peak = jnp.take(peak, slot_pick, axis=0)
    factor = jnp.exp(got_max - device_peak)
    cache_total = jnp.einsum(
        "dg,dth->gth", match_float, got_total * factor, precision=lax.Precision.HIGHEST
    )
    scaled_sum = got_sum.reshape(blk_count, slot_rows, head_count, DH) * factor[..., None]
    cache_sum = jnp.einsum(
        "dg,dthe->gthe", match_float, scaled_sum, precision=lax.Precision.HIGHEST
    )
    self_factor = jnp.exp(self_peak - peak)
    numerator = cache_sum + self_sum * self_factor[..., None]
    denominator = cache_total + self_total * self_factor
    attended = (
        (numerator / denominator[..., None]).reshape(row_count, col_count).astype(jnp.bfloat16)
    )
    partial_update = jnp.dot(attended, w_out, preferred_element_type=jnp.float32)
    x_float = doc_x.astype(jnp.float32)
    whole_sum = lax.psum(partial_update, "head")
    hidden = x_float + whole_sum
    square_sum = jnp.sum(hidden * hidden, axis=1)
    weighted = jnp.sum(hidden * norm_gain * readout, axis=1)
    update = lax.dynamic_slice_in_dim(whole_sum, head_index * col_count, col_count, 1)
    token_score = weighted * lax.rsqrt(square_sum / D + 1e-06)
    pooled_sum = jnp.dot(token_score, member.astype(jnp.float32), precision=lax.Precision.HIGHEST)
    return (update, pooled_sum / lengths.astype(jnp.float32))


def solution(mesh):
    return jax.shard_map(
        body,
        mesh=mesh,
        in_specs=(
            P("blk", None),
            P("blk"),
            P(),
            P("blk"),
            P(),
            P(),
            P("blk", "head"),
            P("blk", "head"),
            P("blk"),
            P(None, "head"),
            P(None, "head"),
            P(None, "head"),
            P("head", None),
            P(None, "head"),
            P(),
            P(),
        ),
        out_specs=(P("blk", "head"), P("blk")),
        check_vma=False,
    )
```

profile of v0, /device:TPU:1, one launch (start us, length us, event | category | flops | bytes accessed | tf_op | source)
XLA Modules:
  0.0 646.7 jit_solution(2000789111802115484)
XLA Ops:
  11.0 13.2 %all-to-all-start.1 = ((bf16[64,1,128]{2,1,0:T(2,128)(2,1)}), bf16[64,1,128]{2,1,0:T(2,128)(2,1)S(1)}, u32[]{:S(2)}, u32[]{:S(2)}) async-start(bf16[64,1,128]{2,1,0:T(2,128)(2,1)} %copy.100), calls=%async_computation.1 | async-start | bytes 65536 | tf_op jit(solution)/shard_map/all_to_all | solution.py:165
  30.1 2.8 gather_fusion
  32.8 4.6 broadcast_select_fusion
  37.4 10.7 %all-to-all-start = ((bf16[64,128,256]{2,1,0:T(8,128)(2,1)}), bf16[64,128,256]{2,1,0:T(8,128)(2,1)}, u32[]{:S(2)}, u32[]{:S(2)}) async-start(bf16[64,128,256]{2,1,0:T(8,128)(2,1)} %broadcast_select_fusion), calls=%async_computation | async-start | bytes 8388608 | tf_op jit(solution)/shard_map/all_to_all | solution.py:164
  53.1 90.9 %all-to-all-done = bf16[64,128,256]{2,1,0:T(8,128)(2,1)} async-done(((bf16[64,128,256]{2,1,0:T(8,128)(2,1)}), bf16[64,128,256]{2,1,0:T(8,128)(2,1)}, u32[]{:S(2)}, u32[]{:S(2)}) %all-to-all-start) | async-done | bytes 4194336 | tf_op jit(solution)/shard_map/all_to_all | solution.py:164
  144.0 12.9 %reshape.307 = bf16[16,512,4,64]{3,2,1,0:T(4,128)(2,1)} reshape(bf16[64,128,256]{2,1,0:T(8,128)(2,1)} %all-to-all-done) | data formatting | bytes 8388608 | tf_op jit(solution)/shard_map/reshape | solution.py:49
  156.9 12.7 %copy.102 = bf16[16,512,4,64]{1,3,2,0:T(8,128)(2,1)} copy(bf16[16,512,4,64]{3,2,1,0:T(4,128)(2,1)} %reshape.307) | data formatting | bytes 8388608
  169.6 122.0 %while.15 = (s32[]{:T(128)}, f32[16,512,4]{1,2,0:T(4,128)S(1)}, f32[16,512,4]{1,2,0:T(4,128)S(1)}, f32[16,512,256]{2,1,0:T(8,128)}, bf16[16,512,4,64]{1,3,2,0:T(...) while((s32[]{:T(128)}, f32[16,512,4]{1,2,0:T(4,128)S(1)}, ...), condition=%wide.region_7.8_spmd.clone, body=%wide.region_4.7_spmd.clone.sunk | while | flops 288617472 | bytes 17115396 | solution.py:68
  170.6 2.5 fusion.87
  193.5 2.5 fusion.87
  201.1 2.5 fusion.87
  208.7 2.5 fusion.87
  216.3 2.5 fusion.87
  223.9 2.5 fusion.87
  231.5 2.5 fusion.87
  246.8 2.5 fusion.87
  254.4 2.5 fusion.87
  262.0 2.5 fusion.87
  277.3 2.5 fusion.87
  284.9 2.5 fusion.87
  291.6 16.0 %all_to_all.26 = f32[64,128,4]{1,2,0:T(4,128)} all-to-all(f32[64,128,4]{1,2,0:T(4,128)S(1)} %bitcast.155), channel_id=1, replica_groups=mesh['head'=4,'blk'=64] {'blk'}, dimensions={0} | all-to-all | bytes 262144 | tf_op jit(solution)/shard_map/all_to_all | solution.py:172
  307.6 15.0 %all_to_all.27 = f32[64,128,4]{1,2,0:T(4,128)S(1)} all-to-all(f32[64,128,4]{1,2,0:T(4,128)S(1)} %bitcast.154), channel_id=1, replica_groups=mesh['head'=4,'blk'=64] {'blk'}, dimensions={0} | all-to-all | bytes 262144 | tf_op jit(solution)/shard_map/all_to_all | solution.py:171
  322.6 5.6 all-to-all-start.2
  330.0 2.5 convolution_convert_fusion
  332.5 2.8 reshape.308
  342.1 172.0 %all-to-all-done.2 = f32[64,128,256]{2,1,0:T(8,128)} async-done(((f32[64,128,256]{2,1,0:T(8,128)}), f32[64,128,256]{2,1,0:T(8,128)}, u32[]{:S(2)}, u32[]{:S(2)}) %all-to-all-start.2) | async-done | bytes 8388640 | tf_op jit(solution)/shard_map/all_to_all | solution.py:173
  514.1 9.0 %copy.104 = f32[64,128,256]{1,2,0:T(8,128)} copy(f32[64,128,256]{2,1,0:T(8,128)} %all-to-all-done.2) | data formatting | bytes 16777216 | tf_op jit(solution)/shard_map/all_to_all | solution.py:173
  523.0 4.6 broadcast_multiply_fusion
  527.7 8.5 %fusion.24 = bf16[8,128,4,64]{1,0,3,2:T(8,128)(2,1)S(1)} fusion(f32[64,128,4,64]{1,3,2,0:T(8,128)S(1)} %broadcast_multiply_fusion, f32[8,4,64,128]{3,2,1,0:T(8,128)S(1)} %copy-done.3, f32[8,128,4]{1,0,2:T(8,128)S(1)} %convolution_add_fusion, f32[8,128,4]{1,0,2:T(8,128)S(1)} %get-tuple-element.189, s32[64]{0:T(128)S(1)} %copy-done.16, s32[8]{0:T(128)S(1)} %copy-done.13), kind=kOutput, calls=%fused_computation.36 | convolution fusion | flops 202375680 | bytes 9994528 | tf_op jit(solution)/shard_map/dg,dthe->gthe/dot_general | solution.py:185
  536.2 2.7 fusion.34
  539.0 94.6 %all-reduce.2.cloned.1.call-done = f32[1024,1024]{1,0:T(8,128)} async-done(((f32[1024,1024]{1,0:T(8,128)}), f32[1024,1024]{1,0:T(8,128)}) %all-reduce.2.cloned.1.call-update) | async-done | bytes 4194320 | tf_op jit(solution)/shard_map/psum | solution.py:196
  633.6 3.3 multiply_reduce_fusion
  (247 shorter events, 115.1 us)
Async XLA Ops:
  7.2 529.0 %copy-start = (bf16[256,1024]{1,0:T(8,128)(2,1)S(1)}, bf16[256,1024]{1,0:T(8,128)(2,1)}, u32[]{:S(2)}) copy-start(bf16[256,1024]{1,0:T(8,128)(2,1)} %param.30) | copy-start | bytes 1572868
  7.9 320.7 %copy-start.15 = (s32[64]{0:T(128)}, s32[64]{0:T(128)S(1)}, u32[]{:S(2)}) copy-start(s32[64]{0:T(128)S(1)} %and_select_fusion) | copy-start | bytes 772
  8.9 319.7 %copy-start.12 = (s32[8]{0:T(128)}, s32[8]{0:T(128)S(1)}, u32[]{:S(2)}) copy-start(s32[8]{0:T(128)S(1)} %slice_reduce_fusion) | copy-start | bytes 100
  9.0 23.9 %copy-start.17 = (pred[64]{0:T(512)(128)(4,1)}, pred[64]{0:T(512)(128)(4,1)S(1)}, u32[]{:S(2)}) copy-start(pred[64]{0:T(512)(128)(4,1)S(1)} %compare_and_fusion) | copy-start | bytes 196
  9.0 21.1 %copy-start.14 = (s32[1024]{0:T(1024)}, s32[1024]{0:T(1024)S(1)}, u32[]{:S(2)}) copy-start(s32[1024]{0:T(1024)S(1)} %pad_clamp_fusion) | copy-start | bytes 12292
  11.0 26.4 %all-to-all-start.1 = ((bf16[64,1,128]{2,1,0:T(2,128)(2,1)}), bf16[64,1,128]{2,1,0:T(2,128)(2,1)S(1)}, u32[]{:S(2)}, u32[]{:S(2)}) async-start(bf16[64,1,128]{2,1,0:T(2,128)(2,1)} %copy.100), calls=%async_computation.1 | async-start | bytes 65536 | tf_op jit(solution)/shard_map/all_to_all | solution.py:165
  24.9 4.8 copy-start.10
  25.0 0.5 copy-start.21
  37.4 10.7 %copy-start.26 = (s32[64]{0:T(128)S(1)}, s32[64]{0:T(128)}, u32[]{:S(2)}) copy-start(s32[64]{0:T(128)} %param.23) | copy-start | bytes 772
  37.4 13.9 %copy-start.6 = (bf16[512,256]{1,0:T(8,128)(2,1)S(1)}, bf16[512,256]{1,0:T(8,128)(2,1)}, u32[]{:S(2)}) copy-start(bf16[512,256]{1,0:T(8,128)(2,1)} %param.24) | copy-start | bytes 786436
  37.4 14.1 %copy-start.7 = (bf16[512,256]{1,0:T(8,128)(2,1)S(1)}, bf16[512,256]{1,0:T(8,128)(2,1)}, u32[]{:S(2)}) copy-start(bf16[512,256]{1,0:T(8,128)(2,1)} %param.25) | copy-start | bytes 786436
  37.4 14.3 %copy-start.27 = (s32[8]{0:T(128)S(1)}, s32[8]{0:T(128)}, u32[]{:S(2)}) copy-start(s32[8]{0:T(128)} %param.22) | copy-start | bytes 100
  37.4 14.9 %copy-start.23 = (f32[2,4]{1,0:T(2,128)S(1)}, f32[2,4]{1,0:T(2,128)}, u32[]{:S(2)}) copy-start(f32[2,4]{1,0:T(2,128)} %param.31) | copy-start | bytes 100
  37.4 106.5 %all-to-all-start = ((bf16[64,128,256]{2,1,0:T(8,128)(2,1)}), bf16[64,128,256]{2,1,0:T(8,128)(2,1)}, u32[]{:S(2)}, u32[]{:S(2)}) async-start(bf16[64,128,256]{2,1,0:T(8,128)(2,1)} %broadcast_select_fusion), calls=%async_computation | async-start | bytes 8388608 | tf_op jit(solution)/shard_map/all_to_all | solution.py:164
  156.9 12.7 %copy-start.8 = (s32[512]{0:T(512)S(1)}, s32[512]{0:T(512)}, u32[]{:S(2)}) copy-start(s32[512]{0:T(512)} %param.26) | copy-start | bytes 6148
  322.6 7.4 %copy-start.1 = (bf16[1024,1024]{1,0:T(8,128)(2,1)S(1)}, bf16[1024,1024]{1,0:T(8,128)(2,1)}, u32[]{:S(2)}) copy-start(bf16[1024,1024]{1,0:T(8,128)(2,1)} %param.18) | copy-start | bytes 6291460
  322.6 191.5 %all-to-all-start.2 = ((f32[64,128,256]{2,1,0:T(8,128)}), f32[64,128,256]{2,1,0:T(8,128)}, u32[]{:S(2)}, u32[]{:S(2)}) async-start(f32[64,128,256]{2,1,0:T(8,128)} %bitcast.145), calls=%async_computation.2 | async-start | bytes 16777216 | tf_op jit(solution)/shard_map/all_to_all | solution.py:173
  328.3 7.0 %copy-start.9 = (s32[1024]{0:T(1024)S(1)}, s32[1024]{0:T(1024)}, u32[]{:S(2)}) copy-start(s32[1024]{0:T(1024)} %param.19) | copy-start | bytes 12292
  328.3 7.0 %copy-start.2 = (s32[1024]{0:T(1024)S(1)}, s32[1024]{0:T(1024)}, u32[]{:S(2)}) copy-start(s32[1024]{0:T(1024)} %param.21) | copy-start | bytes 12292
  328.3 305.3 %all-reduce.2.cloned.1.call-start = ((), (), s32[]{:S(2)}) async-start(), calls=%async_computation.5 | async-start | bytes 8388608 | tf_op jit(solution)/shard_map/psum | solution.py:196
  335.3 2.4 copy-start.24
  335.3 2.4 copy-start.25
  337.7 1.3 copy-start.4
  340.8 1.0 copy-start.5
  340.8 1.0 copy-start.18
  340.8 1.1 copy-start.13
  340.8 1.1 copy-start.16
  523.0 4.7 copy-start.3
  538.9 94.7 %copy-start.19 = (f32[1024]{0:T(1024)S(1)}, f32[1024]{0:T(1024)}, u32[]{:S(2)}) copy-start(f32[1024]{0:T(1024)} %param.33) | copy-start | bytes 12292
  538.9 94.7 %copy-start.20 = (f32[1024]{0:T(1024)S(1)}, f32[1024]{0:T(1024)}, u32[]{:S(2)}) copy-start(f32[1024]{0:T(1024)} %param.32) | copy-start | bytes 12292
  539.0 97.9 %copy-start.11 = (s32[1024]{0:T(1024)S(1)}, s32[1024]{0:T(1024)}, u32[]{:S(2)}) copy-start(s32[1024]{0:T(1024)} %copy-done.10) | copy-start | bytes 12292
  539.0 97.9 %copy-start.22 = (s32[16]{0:T(128)S(1)}, s32[16]{0:T(128)}, u32[]{:S(2)}) copy-start(s32[16]{0:T(128)} %copy-done.21) | copy-start | bytes 196
Sparse Core Ops, SparseCore 0:
  539.1 94.4 all-reduce.1
where the time goes:
time: 649 us; the launch traced here: 647 us
  waiting for transfers between devices  358 us (55%)
  matrix products  87.6 us (13%)
  local copies, waits for them, and re-layouts  66.9 us (10%)
  other arithmetic  56 us (9%)
  blocking collectives  31 us (5%)
  starting transfers between devices  29.7 us (5%)
  between operations  17.2 us (3%)
    all_to_all x1, waiting for transfers between devices, body(): lax.all_to_all(sums, 'blk', split_axis=0, concat_axis=0, tiled=True)  172 us
    psum x1, waiting for transfers between devices, body(): whole_sum = lax.psum(partial_update, 'head')  94.6 us
    all_to_all x1, waiting for transfers between devices, body(): lax.all_to_all(send_q, 'blk', split_axis=0, concat_axis=0, tiled=True)  90.9 us
    dot_general x16, matrix products, one_block(): jnp.einsum('thd,rhd->htr', block_q, cache_keys, preferred_element_type=jn...  39.2 us
    dot_general x16, matrix products, one_block(): jnp.einsum('htr,rhd->thd', weights, cache_values, preferred_element_type=...  26.9 us
    reduce_sum x17, other arithmetic, softmax_part(): return (peak, jnp.sum(weights, axis=-1), weights.astype(jnp.bfloat16))  24 us
    dynamic_update_slice x48, local copies, waits for them, and re-layouts, cache_part(): maxima, totals, sums = lax.map(one_block, (flat_q, flat_var))  16.9 us
    all_to_all x1, blocking collectives, body(): lax.all_to_all(totals, 'blk', split_axis=0, concat_axis=0, tiled=True)  16 us
  transfers between devices with their start and end apart: 4, of which 3 were waited for; matrix products, arithmetic and copies ran while one was open for 4% of the time, Pallas kernels for 0%

commit v1 on v0

--- a/solution.py
+++ b/solution.py
@@ -193,7 +193,11 @@
     )
     partial_update = jnp.dot(attended, w_out, preferred_element_type=jnp.float32)
     x_float = doc_x.astype(jnp.float32)
-    whole_sum = lax.psum(partial_update, "head")
+    size = lax.axis_size("head")
+    whole_sum, hop = (partial_update, 1)
+    while hop < size:
+        whole_sum = whole_sum + lax.ppermute(whole_sum, "head", [(i, i ^ hop) for i in range(size)])
+        hop = 2 * hop
     hidden = x_float + whole_sum
     square_sum = jnp.sum(hidden * hidden, axis=1)
     weighted = jnp.sum(hidden * norm_gain * readout, axis=1)

time: 649 us -> 726 us (1.12)
  waiting for transfers between devices: 358 us -> 442 us
  between operations: 17.2 us -> 3.8 us
    ppermute x0 -> x2, waiting for transfers between devices: none -> 179 us  [body(): lax.ppermute(whole_sum, 'head', [(i, i ^ hop) for i in range(size)])]
    psum x1 -> x0, waiting for transfers between devices: 94.6 us -> none  [body(): whole_sum = lax.psum(partial_update, 'head')]
    unnamed x60 -> x62, local copies, waits for them, and re-layouts: 13.3 us -> 17.2 us
  transfers between devices with their start and end apart: 4 -> 5, of which waited for: 3 -> 4; matrix products, arithmetic and copies ran while one was open for 4% -> 4% of each run, Pallas kernels for 0% -> 0%
where the time goes in v1:
time: 726 us; the launch traced here: 724 us
  waiting for transfers between devices  442 us (61%)
  matrix products  85.7 us (12%)
  local copies, waits for them, and re-layouts  68.5 us (9%)
  other arithmetic  58 us (8%)
  starting transfers between devices  33.8 us (5%)
  blocking collectives  31 us (4%)
    ppermute x2, waiting for transfers between devices, body(): lax.ppermute(whole_sum, 'head', [(i, i ^ hop) for i in range(size)])  179 us
    all_to_all x1, waiting for transfers between devices, body(): lax.all_to_all(sums, 'blk', split_axis=0, concat_axis=0, tiled=True)  172 us
    all_to_all x1, waiting for transfers between devices, body(): lax.all_to_all(send_q, 'blk', split_axis=0, concat_axis=0, tiled=True)  91 us
    dot_general x16, matrix products, one_block(): jnp.einsum('thd,rhd->htr', block_q, cache_keys, preferred_element_type=jn...  39.2 us
    dot_general x16, matrix products, one_block(): jnp.einsum('htr,rhd->thd', weights, cache_values, preferred_element_type=...  26.9 us
    reduce_sum x17, other arithmetic, softmax_part(): return (peak, jnp.sum(weights, axis=-1), weights.astype(jnp.bfloat16))  24 us
    unnamed x62, local copies, waits for them, and re-layouts  17.2 us
    dynamic_update_slice x48, local copies, waits for them, and re-layouts, cache_part(): maxima, totals, sums = lax.map(one_block, (flat_q, flat_var))  16.9 us
  transfers between devices with their start and end apart: 5, of which 4 were waited for; matrix products, arithmetic and copies ran while one was open for 4% of the time, Pallas kernels for 0%

profile of v1, /device:TPU:1, one launch (start us, length us, event | category | flops | bytes accessed | tf_op | source)
XLA Modules:
  0.0 724.0 jit_solution(5790719046161424733)
XLA Ops:
  4.5 13.2 %all-to-all-start.1 = ((bf16[64,1,128]{2,1,0:T(2,128)(2,1)}), bf16[64,1,128]{2,1,0:T(2,128)(2,1)S(1)}, u32[]{:S(2)}, u32[]{:S(2)}) async-start(bf16[64,1,128]{2,1,0:T(2,128)(2,1)} %copy.108), calls=%async_computation.1 | async-start | bytes 65536 | tf_op jit(solution)/shard_map/all_to_all | solution.py:165
  23.5 2.7 gather_fusion
  26.3 4.6 broadcast_select_fusion
  30.9 10.7 %all-to-all-start = ((bf16[64,128,256]{2,1,0:T(8,128)(2,1)}), bf16[64,128,256]{2,1,0:T(8,128)(2,1)}, u32[]{:S(2)}, u32[]{:S(2)}) async-start(bf16[64,128,256]{2,1,0:T(8,128)(2,1)} %broadcast_select_fusion), calls=%async_computation | async-start | bytes 8388608 | tf_op jit(solution)/shard_map/all_to_all | solution.py:164
  46.4 91.0 %all-to-all-done = bf16[64,128,256]{2,1,0:T(8,128)(2,1)} async-done(((bf16[64,128,256]{2,1,0:T(8,128)(2,1)}), bf16[64,128,256]{2,1,0:T(8,128)(2,1)}, u32[]{:S(2)}, u32[]{:S(2)}) %all-to-all-start) | async-done | bytes 4194336 | tf_op jit(solution)/shard_map/all_to_all | solution.py:164
  137.4 12.9 %reshape.307 = bf16[16,512,4,64]{3,2,1,0:T(4,128)(2,1)} reshape(bf16[64,128,256]{2,1,0:T(8,128)(2,1)} %all-to-all-done) | data formatting | bytes 8388608 | tf_op jit(solution)/shard_map/reshape | solution.py:49
  150.3 12.7 %copy.110 = bf16[16,512,4,64]{1,3,2,0:T(8,128)(2,1)} copy(bf16[16,512,4,64]{3,2,1,0:T(4,128)(2,1)} %reshape.307) | data formatting | bytes 8388608
  163.0 119.6 %while.15 = (s32[]{:T(128)}, f32[16,512,4]{1,2,0:T(4,128)S(1)}, f32[16,512,4]{1,2,0:T(4,128)S(1)}, f32[16,512,256]{2,1,0:T(8,128)}, bf16[16,512,4,64]{1,3,2,0:T(...) while((s32[]{:T(128)}, f32[16,512,4]{1,2,0:T(4,128)S(1)}, ...), condition=%wide.region_7.8_spmd.clone, body=%wide.region_4.7_spmd.clone.sunk | while | flops 288617472 | bytes 17115396 | solution.py:68
  163.8 2.5 fusion.87
  171.4 2.5 fusion.87
  193.8 2.5 fusion.87
  208.7 2.5 fusion.87
  216.2 2.5 fusion.87
  231.1 2.5 fusion.87
  253.5 2.5 fusion.87
  261.0 2.5 fusion.87
  276.0 2.5 fusion.87
  282.7 16.0 %all_to_all.26 = f32[64,128,4]{1,2,0:T(4,128)} all-to-all(f32[64,128,4]{1,2,0:T(4,128)S(1)} %bitcast.155), channel_id=1, replica_groups=mesh['head'=4,'blk'=64] {'blk'}, dimensions={0} | all-to-all | bytes 262144 | tf_op jit(solution)/shard_map/all_to_all | solution.py:172
  298.7 15.0 %all_to_all.27 = f32[64,128,4]{1,2,0:T(4,128)S(1)} all-to-all(f32[64,128,4]{1,2,0:T(4,128)S(1)} %bitcast.154), channel_id=1, replica_groups=mesh['head'=4,'blk'=64] {'blk'}, dimensions={0} | all-to-all | bytes 262144 | tf_op jit(solution)/shard_map/all_to_all | solution.py:171
  313.7 5.7 all-to-all-start.2
  320.8 2.6 convolution_convert_fusion
  323.4 2.8 reshape.308
  333.0 172.2 %all-to-all-done.2 = f32[64,128,256]{2,1,0:T(8,128)} async-done(((f32[64,128,256]{2,1,0:T(8,128)}), f32[64,128,256]{2,1,0:T(8,128)}, u32[]{:S(2)}, u32[]{:S(2)}) %all-to-all-start.2) | async-done | bytes 8388640 | tf_op jit(solution)/shard_map/all_to_all | solution.py:173
  505.1 9.0 %copy.112 = f32[64,128,256]{1,2,0:T(8,128)} copy(f32[64,128,256]{2,1,0:T(8,128)} %all-to-all-done.2) | data formatting | bytes 16777216 | tf_op jit(solution)/shard_map/all_to_all | solution.py:173
  514.1 4.6 broadcast_multiply_fusion
  518.8 8.5 %fusion.24 = bf16[8,128,4,64]{1,0,3,2:T(8,128)(2,1)S(1)} fusion(f32[64,128,4,64]{1,3,2,0:T(8,128)S(1)} %broadcast_multiply_fusion, f32[8,4,64,128]{3,2,1,0:T(8,128)S(1)} %copy-done.3, f32[8,128,4]{1,0,2:T(8,128)S(1)} %convolution_add_fusion, f32[8,128,4]{1,0,2:T(8,128)S(1)} %get-tuple-element.200, s32[64]{0:T(128)S(1)} %copy-done.16, s32[8]{0:T(128)S(1)} %copy-done.13), kind=kOutput, calls=%fused_computation.36 | convolution fusion | flops 202375680 | bytes 9994528 | tf_op jit(solution)/shard_map/dg,dthe->gthe/dot_general | solution.py:185
  529.6 91.2 %collective-permute-done = f32[1024,1024]{0,1:T(8,128)S(1)} collective-permute-done((f32[1024,1024]{0,1:T(8,128)S(1)}, f32[1024,1024]{0,1:T(8,128)S(1)}, u32[]{:S(2)}, u32[]{:S(2)}) %collective-permute-start) | collective-permute-done | bytes 4194336 | tf_op jit(solution)/shard_map/ppermute | solution.py:199
  620.8 2.9 add.102
  623.7 2.7 collective-permute-start.1
  626.4 2.6 copy.125
  629.0 88.1 %collective-permute-done.1 = f32[1024,1024]{0,1:T(8,128)} collective-permute-done((f32[1024,1024]{0,1:T(8,128)}, f32[1024,1024]{0,1:T(8,128)}, u32[]{:S(2)}, u32[]{:S(2)}) %collective-permute-start.1) | collective-permute-done | bytes 4194336 | tf_op jit(solution)/shard_map/ppermute | solution.py:199
  717.1 4.8 multiply_reduce_fusion
  (251 shorter events, 121.1 us)
Async XLA Ops:
  0.6 526.7 %copy-start = (bf16[256,1024]{1,0:T(8,128)(2,1)S(1)}, bf16[256,1024]{1,0:T(8,128)(2,1)}, u32[]{:S(2)}) copy-start(bf16[256,1024]{1,0:T(8,128)(2,1)} %param.30) | copy-start | bytes 1572868
  1.4 318.0 %copy-start.15 = (s32[64]{0:T(128)}, s32[64]{0:T(128)S(1)}, u32[]{:S(2)}) copy-start(s32[64]{0:T(128)S(1)} %and_select_fusion) | copy-start | bytes 772
  2.3 317.1 %copy-start.12 = (s32[8]{0:T(128)}, s32[8]{0:T(128)S(1)}, u32[]{:S(2)}) copy-start(s32[8]{0:T(128)S(1)} %slice_reduce_fusion) | copy-start | bytes 100
  2.4 23.8 %copy-start.17 = (pred[64]{0:T(512)(128)(4,1)}, pred[64]{0:T(512)(128)(4,1)S(1)}, u32[]{:S(2)}) copy-start(pred[64]{0:T(512)(128)(4,1)S(1)} %compare_and_fusion) | copy-start | bytes 196
  2.5 21.1 %copy-start.14 = (s32[1024]{0:T(1024)}, s32[1024]{0:T(1024)S(1)}, u32[]{:S(2)}) copy-start(s32[1024]{0:T(1024)S(1)} %pad_clamp_fusion) | copy-start | bytes 12292
  4.5 26.4 %all-to-all-start.1 = ((bf16[64,1,128]{2,1,0:T(2,128)(2,1)}), bf16[64,1,128]{2,1,0:T(2,128)(2,1)S(1)}, u32[]{:S(2)}, u32[]{:S(2)}) async-start(bf16[64,1,128]{2,1,0:T(2,128)(2,1)} %copy.108), calls=%async_computation.1 | async-start | bytes 65536 | tf_op jit(solution)/shard_map/all_to_all | solution.py:165
  18.4 4.8 copy-start.10
  30.8 10.7 %copy-start.26 = (s32[64]{0:T(128)S(1)}, s32[64]{0:T(128)}, u32[]{:S(2)}) copy-start(s32[64]{0:T(128)} %param.23) | copy-start | bytes 772
  30.8 13.9 %copy-start.6 = (bf16[512,256]{1,0:T(8,128)(2,1)S(1)}, bf16[512,256]{1,0:T(8,128)(2,1)}, u32[]{:S(2)}) copy-start(bf16[512,256]{1,0:T(8,128)(2,1)} %param.24) | copy-start | bytes 786436
  30.8 14.1 %copy-start.7 = (bf16[512,256]{1,0:T(8,128)(2,1)S(1)}, bf16[512,256]{1,0:T(8,128)(2,1)}, u32[]{:S(2)}) copy-start(bf16[512,256]{1,0:T(8,128)(2,1)} %param.25) | copy-start | bytes 786436
  30.8 14.3 %copy-start.27 = (s32[8]{0:T(128)S(1)}, s32[8]{0:T(128)}, u32[]{:S(2)}) copy-start(s32[8]{0:T(128)} %param.22) | copy-start | bytes 100
  30.8 14.8 %copy-start.23 = (f32[2,4]{1,0:T(2,128)S(1)}, f32[2,4]{1,0:T(2,128)}, u32[]{:S(2)}) copy-start(f32[2,4]{1,0:T(2,128)} %param.31) | copy-start | bytes 100
  30.9 106.5 %all-to-all-start = ((bf16[64,128,256]{2,1,0:T(8,128)(2,1)}), bf16[64,128,256]{2,1,0:T(8,128)(2,1)}, u32[]{:S(2)}, u32[]{:S(2)}) async-start(bf16[64,128,256]{2,1,0:T(8,128)(2,1)} %broadcast_select_fusion), calls=%async_computation | async-start | bytes 8388608 | tf_op jit(solution)/shard_map/all_to_all | solution.py:164
  150.3 12.7 %copy-start.8 = (s32[512]{0:T(512)S(1)}, s32[512]{0:T(512)}, u32[]{:S(2)}) copy-start(s32[512]{0:T(512)} %param.26) | copy-start | bytes 6148
  313.7 7.2 copy-start.1
  313.7 191.5 %all-to-all-start.2 = ((f32[64,128,256]{2,1,0:T(8,128)}), f32[64,128,256]{2,1,0:T(8,128)}, u32[]{:S(2)}, u32[]{:S(2)}) async-start(f32[64,128,256]{2,1,0:T(8,128)} %bitcast.145), calls=%async_computation.2 | async-start | bytes 16777216 | tf_op jit(solution)/shard_map/all_to_all | solution.py:173
  319.4 6.8 copy-start.9
  319.4 6.8 copy-start.2
  326.1 2.4 copy-start.24
  326.2 2.4 copy-start.25
  328.6 1.3 copy-start.4
  331.6 1.0 copy-start.5
  331.6 1.0 copy-start.18
  331.6 1.1 copy-start.13
  331.6 1.1 copy-start.16
  514.1 4.7 copy-start.3
  528.1 92.8 %collective-permute-start = (f32[1024,1024]{0,1:T(8,128)S(1)}, f32[1024,1024]{0,1:T(8,128)S(1)}, u32[]{:S(2)}, u32[]{:S(2)}) collective-permute-start(f32[1024,1024]{0,1:T(8,128)S(1)} %fusion.34), channel_id=1, source_target_pairs={{0,64},{64,0},{128,192},{192,128},{1,65},{65,1},{129,193},{193,129... | collective-permute-start | bytes 12582920 | tf_op jit(solution)/shard_map/ppermute | solution.py:199
  623.7 93.4 %copy-start.19 = (f32[1024]{0:T(1024)S(1)}, f32[1024]{0:T(1024)}, u32[]{:S(2)}) copy-start(f32[1024]{0:T(1024)} %param.33) | copy-start | bytes 12292
  623.7 93.4 %copy-start.20 = (f32[1024]{0:T(1024)S(1)}, f32[1024]{0:T(1024)}, u32[]{:S(2)}) copy-start(f32[1024]{0:T(1024)} %param.32) | copy-start | bytes 12292
  623.7 93.4 %collective-permute-start.1 = (f32[1024,1024]{0,1:T(8,128)}, f32[1024,1024]{0,1:T(8,128)}, u32[]{:S(2)}, u32[]{:S(2)}) collective-permute-start(f32[1024,1024]{0,1:T(8,128)} %add.102), channel_id=1, source_target_pairs={{0,128},{64,192},{128,0},{192,64},{1,129},{65,193},{129,1},{193,65... | collective-permute-start | bytes 12582920 | tf_op jit(solution)/shard_map/ppermute | solution.py:199
  721.8 1.4 copy-start.11
  721.9 1.4 copy-start.22
  (1 other events, 0.5 us)
